TPU v7x, 32 devices: a whole 2x2x4 slice. The times are simulated.
32 devices in a mesh: seg: 2 (over y), row: 8 (over z, x), col: 2 (over core).
Axes of the slice: x: 2, y: 2, z: 4, core: 2. Of those that a mesh axis runs over, the one named last changes fastest.
Arguments:
- slices: bfloat16 [4, 4096, 4096], P('col', 'seg', 'row'), may hold values from -1 to 1
Outputs:
- prefixes: bfloat16 [4, 4096, 4096], P('col', 'seg', 'row')
All inputs are finite; a program needn't handle non-finite values.
Results may differ from a plain program's by a relative error of at most 0.004.
Values may be sent and summed in bfloat16 or wider, within the bound.
No kernel may reach another device: no remote copies, remote signals or barrier semaphores. Data moves between devices by JAX's collectives and lax.ppermute only.
A program may use at most 128 MiB of HBM per device.

v0:
```python
import math
import jax
import jax.numpy as jnp
from jax import lax
from jax.sharding import PartitionSpec as P

ORDER = 4096


def passed_along(value, axis, by):
    count = lax.axis_size(axis)
    pairs = [(i, i + by) for i in range(count) if 0 <= i + by < count]
    return lax.ppermute(value, axis, pairs)


def column_panel(tile):
    return lax.all_gather(tile, "seg", axis=0, tiled=True)


def times_panel(left_tile, right_block):
    gathered = lax.all_gather(left_tile, "row", axis=1, tiled=True)
    return jnp.dot(gathered, right_block, preferred_element_type=jnp.float32)


def earlier_panel(tile, distance):
    return passed_along(column_panel(tile), "col", distance)


def local(slices):
    group_index = lax.axis_index("col")
    group_count = lax.axis_size("col")
    history = [slices[0]]
    history.append(times_panel(slices[1], column_panel(history[-1])).astype(jnp.bfloat16))
    running = history[-1]
    distance = 1
    while distance < group_count:
        product = times_panel(running, earlier_panel(running, distance)).astype(jnp.bfloat16)
        running = jnp.where(group_index >= distance, product, running)
        distance = distance * 2
    carried_block = earlier_panel(running, 1)
    factor = math.sqrt(ORDER)
    results = []
    for local_tile in history:
        applied = times_panel(local_tile, carried_block)
        chosen = jnp.where(group_index > 0, applied, local_tile.astype(jnp.float32))
        results.append((chosen * factor).astype(jnp.bfloat16))
    return jnp.stack(results, axis=0)


def solution(mesh):
    in_specs = (P("col", "seg", "row"),)
    out_specs = P("col", "seg", "row")
    return jax.shard_map(local, mesh=mesh, in_specs=in_specs, out_specs=out_specs, check_vma=False)
```

profile of v0, /device:TPU:0, one launch (start us, length us, event | category | flops | bytes accessed | tf_op | source)
XLA Modules:
  0.0 920.9 jit_solution(10815625901203171808)
XLA Ops:
  6.5 0.0 all-gather.18.cloned.1.call-start
  6.5 4.5 fusion.19
  11.1 0.0 all-gather.18.cloned.1.call-update
  11.1 0.0 all-gather.16.cloned.1.call-start
  11.2 0.7 all-gather.16.cloned.1.call-update
  11.9 0.0 all-gather.12.cloned.1.call-start
  11.9 58.8 %all-gather.18.cloned.1.call-done = bf16[1,4096,512]{2,1,0:T(8,128)(2,1)} async-done(((bf16[1,2048,512]{2,1,0:T(8,128)(2,1)}), bf16[1,4096,512]{2,1,0:T(8,128)(2,1)}) %all-gather.18.cloned.1.call-update) | async-done | bytes 4194320 | tf_op jit(solution)/shard_map/all_gather | solution.py:17
  70.7 229.4 %all-gather.16.cloned.1.call-done = bf16[1,2048,4096]{2,1,0:T(8,128)(2,1)} async-done(((bf16[1,2048,512]{2,1,0:T(8,128)(2,1)}), bf16[1,2048,4096]{2,1,0:T(8,128)(2,1)}) %all-gather.16.cloned.1.call-update) | async-done | bytes 16777232 | tf_op jit(solution)/shard_map/all_gather | solution.py:21
  300.1 14.5 %fusion.9 = bf16[2048,512]{1,0:T(8,128)(2,1)} fusion(bf16[1,4096,512]{2,1,0:T(8,128)(2,1)} %all-gather.18.cloned.1.call-done, bf16[1,2048,4096]{2,1,0:T(8,128)(2,1)} %all-gather.16.cloned.1.call-done), kind=kOutput, calls=%fused_computation.10 | convolution fusion | flops 8590983168 | bytes 23068672 | tf_op jit(solution)/shard_map/dot_general | solution.py:22
  314.6 0.0 copy-start
  314.6 0.0 all-gather.12.cloned.1.call-update
  314.6 0.0 all-gather.10.cloned.1.call-start
  314.7 0.5 all-gather.10.cloned.1.call-update
  315.2 0.0 all-gather.14.cloned.1.call-start
  315.3 54.4 %all-gather.12.cloned.1.call-done = bf16[4096,512]{1,0:T(8,128)(2,1)} async-done(((bf16[2048,512]{1,0:T(8,128)(2,1)}), bf16[4096,512]{1,0:T(8,128)(2,1)}) %all-gather.12.cloned.1.call-update) | async-done | bytes 4194320 | tf_op jit(solution)/shard_map/all_gather | solution.py:17
  369.7 3.6 collective-permute-start
  373.3 5.1 collective-permute-done
  378.4 220.5 %all-gather.10.cloned.1.call-done = bf16[2048,4096]{1,0:T(8,128)(2,1)} async-done(((bf16[2048,512]{1,0:T(8,128)(2,1)}), bf16[2048,4096]{1,0:T(8,128)(2,1)}) %all-gather.10.cloned.1.call-update) | async-done | bytes 16777232 | tf_op jit(solution)/shard_map/all_gather | solution.py:21
  598.9 0.0 copy-done
  598.9 14.5 %fusion.18 = bf16[2048,512]{1,0:T(8,128)(2,1)} fusion(bf16[2048,512]{1,0:T(8,128)(2,1)S(1)} %copy-done, bf16[2048,4096]{1,0:T(8,128)(2,1)} %all-gather.10.cloned.1.call-done, bf16[4096,512]{1,0:T(8,128)(2,1)} %collective-permute-done, pred[]{:T(512)S(6)} %ge.3), kind=kOutput, calls=%fused_computation.14 | convolution fusion | flops 8592031744 | bytes 25165824 | tf_op jit(solution)/shard_map/dot_general | solution.py:22
  613.5 0.0 all-gather.14.cloned.1.call-update
  613.5 0.0 all-gather.20.cloned.1.call-start
  613.5 0.5 all-gather.20.cloned.1.call-update
  614.1 54.5 %all-gather.14.cloned.1.call-done = bf16[4096,512]{1,0:T(8,128)(2,1)} async-done(((bf16[2048,512]{1,0:T(8,128)(2,1)}), bf16[4096,512]{1,0:T(8,128)(2,1)}) %all-gather.14.cloned.1.call-update) | async-done | bytes 4194320 | tf_op jit(solution)/shard_map/all_gather | solution.py:17
  668.6 3.6 collective-permute-start.1
  672.2 5.0 collective-permute-done.1
  677.2 15.9 %fusion.14 = bf16[1,2048,512]{2,1,0:T(8,128)(2,1)} fusion(bf16[2048,512]{1,0:T(8,128)(2,1)S(1)} %copy-done, bf16[2048,4096]{1,0:T(8,128)(2,1)} %all-gather.10.cloned.1.call-done, bf16[4096,512]{1,0:T(8,128)(2,1)} %collective-permute-done.1, pred[]{:T(512)S(6)} %gt.4), kind=kOutput, calls=%fused_computation.12 | convolution fusion | flops 8594128896 | bytes 25165824 | tf_op jit(solution)/shard_map/dot_general | solution.py:22
  693.1 0.0 copy-start.1
  693.1 204.6 %all-gather.20.cloned.1.call-done = bf16[1,2048,4096]{2,1,0:T(8,128)(2,1)} async-done(((bf16[1,2048,512]{2,1,0:T(8,128)(2,1)}), bf16[1,2048,4096]{2,1,0:T(8,128)(2,1)}) %all-gather.20.cloned.1.call-update) | async-done | bytes 16777232 | tf_op jit(solution)/shard_map/all_gather | solution.py:21
  897.8 13.9 %fusion.15 = bf16[1,2048,512]{2,1,0:T(8,128)(2,1)S(1)} fusion(bf16[4096,512]{1,0:T(8,128)(2,1)} %collective-permute-done.1, bf16[1,2048,4096]{2,1,0:T(8,128)(2,1)} %all-gather.20.cloned.1.call-done, pred[]{:T(512)S(6)} %gt.4, bf16[2,2048,512]{2,1,0:T(8,128)(2,1)} %param.1), kind=kOutput, calls=%fused_computation.13 | convolution fusion | flops 8594128896 | bytes 25165824 | tf_op jit(solution)/shard_map/dot_general | solution.py:22
  911.7 0.0 copy-done.1
  911.7 2.4 pad_maximum_fusion
Async XLA Ops:
  6.5 64.2 %all-gather.18.cloned.1.call-start = ((), (), s32[]{:S(2)}) async-start(), calls=%async_computation.4 | async-start | bytes 6291456 | tf_op jit(solution)/shard_map/all_gather | solution.py:17
  11.1 289.0 %all-gather.16.cloned.1.call-start = ((), (), s32[]{:S(2)}) async-start(), calls=%async_computation.3 | async-start | bytes 18874368 | tf_op jit(solution)/shard_map/all_gather | solution.py:21
  11.9 357.8 %all-gather.12.cloned.1.call-start = ((), (), s32[]{:S(2)}) async-start(), calls=%async_computation.1 | async-start | bytes 6291456 | tf_op jit(solution)/shard_map/all_gather | solution.py:17
  314.6 284.3 %copy-start = (bf16[2048,512]{1,0:T(8,128)(2,1)S(1)}, bf16[2048,512]{1,0:T(8,128)(2,1)}, u32[]{:S(2)}) copy-start(bf16[2048,512]{1,0:T(8,128)(2,1)} %fusion.9) | copy-start | bytes 6291460
  314.6 284.3 %all-gather.10.cloned.1.call-start = ((), (), s32[]{:S(2)}) async-start(), calls=%async_computation | async-start | bytes 18874368 | tf_op jit(solution)/shard_map/all_gather | solution.py:21
  315.2 353.3 %all-gather.14.cloned.1.call-start = ((), (), s32[]{:S(2)}) async-start(), calls=%async_computation.2 | async-start | bytes 6291456 | tf_op jit(solution)/shard_map/all_gather | solution.py:17
  369.7 8.7 collective-permute-start
  613.5 284.3 %all-gather.20.cloned.1.call-start = ((), (), s32[]{:S(2)}) async-start(), calls=%async_computation.5 | async-start | bytes 18874368 | tf_op jit(solution)/shard_map/all_gather | solution.py:21
  668.6 8.7 collective-permute-start.1
  693.1 218.5 %copy-start.1 = (bf16[1,2048,512]{2,1,0:T(8,128)(2,1)S(1)}, bf16[1,2048,512]{2,1,0:T(8,128)(2,1)}, u32[]{:S(2)}) copy-start(bf16[1,2048,512]{2,1,0:T(8,128)(2,1)} %fusion.14) | copy-start | bytes 6291460
Sparse Core Ops, SparseCore 0:
  11.2 59.4 all-gather.17
  72.8 227.2 all-gather.15
  314.8 54.8 all-gather.11
  371.6 227.2 all-gather.9
  613.6 54.9 all-gather.13
  670.5 227.2 all-gather.19
where the time goes:
time: 921 us
  waiting for transfers between devices  834 us (91%)
  matrix products  58.8 us (6%)
  between operations  13.5 us (1%)
    all_gather x3, waiting for transfers between devices, times_panel(): gathered = lax.all_gather(left_tile, 'row', axis=1, tiled=True)  655 us
    all_gather x3, waiting for transfers between devices, column_panel(): return lax.all_gather(tile, 'seg', axis=0, tiled=True)  168 us
    dot_general x4, matrix products, times_panel(): return jnp.dot(gathered, right_block, preferred_element_type=jnp.float32)  58.8 us
  transfers between devices with their start and end apart: 8, of which 8 were waited for; matrix products, arithmetic and copies ran while one was open for 2% of the time, Pallas kernels for 0%

commit v1 on v0

--- a/solution.py
+++ b/solution.py
@@ -18,7 +18,14 @@
 
 
 def times_panel(left_tile, right_block):
-    gathered = lax.all_gather(left_tile, "row", axis=1, tiled=True)
+    size = lax.axis_size("row")
+    route = [(i_2, (i_2 + 1) % size) for i_2 in range(size)]
+    parts = [left_tile]
+    for reach in range(1, size):
+        parts = [lax.ppermute(parts[0], "row", route), *parts]
+    whole = jnp.concatenate(parts, axis=1)
+    shift = (lax.axis_index("row") + 1) * parts[-1].shape[1]
+    gathered = jnp.roll(whole, shift, axis=1)
     return jnp.dot(gathered, right_block, preferred_element_type=jnp.float32)
 
 

time: 921 us -> 1090 us (1.18)
  waiting for transfers between devices: 834 us -> 925 us
  local copies, waits for them, and re-layouts: 4.55 us -> 73.9 us
    ppermute x0 -> x21, waiting for transfers between devices: none -> 925 us  [times_panel(): parts = [lax.ppermute(parts[0], 'row', route), *parts]]
    all_gather x3 -> x0, waiting for transfers between devices: 655 us -> none  [times_panel(): gathered = lax.all_gather(left_tile, 'row', axis=1, tiled=True)]
    all_gather x3, waiting for transfers between devices: 168 us -> 0.01 us  [column_panel(): return lax.all_gather(tile, 'seg', axis=0, tiled=True)]
    unnamed x4 -> x58, local copies, waits for them, and re-layouts: 0.01 us -> 61.9 us
  transfers between devices with their start and end apart: 8 -> 26, of which waited for: 8 -> 21; matrix products, arithmetic and copies ran while one was open for 2% -> 6% of each run, Pallas kernels for 0% -> 0%
where the time goes in v1:
time: 1090 us
  waiting for transfers between devices  925 us (85%)
  local copies, waits for them, and re-layouts  73.9 us (7%)
  matrix products  61.3 us (6%)
  between operations  13.3 us (1%)
  starting transfers between devices  12.6 us (1%)
    ppermute x21, waiting for transfers between devices, times_panel(): parts = [lax.ppermute(parts[0], 'row', route), *parts]  925 us
    unnamed x58, local copies, waits for them, and re-layouts  61.9 us
    dot_general x4, matrix products, times_panel(): return jnp.dot(gathered, right_block, preferred_element_type=jnp.float32)  61.3 us
  transfers between devices with their start and end apart: 26, of which 21 were waited for; matrix products, arithmetic and copies ran while one was open for 6% of the time, Pallas kernels for 0%

profile of v1, /device:TPU:0, one launch (start us, length us, event | category | flops | bytes accessed | tf_op | source)
XLA Modules:
  0.0 1090.8 jit_solution(268260025311292911)
XLA Ops:
  6.5 2.5 slice_bitcast_fusion
  9.0 3.0 collective-permute-start.7
  12.1 48.7 %collective-permute-done.7 = bf16[2048,512]{1,0:T(8,128)(2,1)S(1)} collective-permute-done((bf16[2048,512]{1,0:T(8,128)(2,1)S(1)}, bf16[2048,512]{1,0:T(8,128)(2,1)S(1)}, u32[]{:S(2)}, u32[]{:S(2)}) %collective-permute-start.7) | collective-permute-done | bytes 2097184 | tf_op jit(solution)/shard_map/ppermute | solution.py:25
  62.1 49.5 %collective-permute-done.8 = bf16[2048,512]{1,0:T(8,128)(2,1)S(1)} collective-permute-done((bf16[2048,512]{1,0:T(8,128)(2,1)S(1)}, bf16[2048,512]{1,0:T(8,128)(2,1)S(1)}, u32[]{:S(2)}, u32[]{:S(2)}) %collective-permute-start.8) | collective-permute-done | bytes 2097184 | tf_op jit(solution)/shard_map/ppermute | solution.py:25
  113.0 48.6 %collective-permute-done.9 = bf16[2048,512]{1,0:T(8,128)(2,1)S(1)} collective-permute-done((bf16[2048,512]{1,0:T(8,128)(2,1)S(1)}, bf16[2048,512]{1,0:T(8,128)(2,1)S(1)}, u32[]{:S(2)}, u32[]{:S(2)}) %collective-permute-start.9) | collective-permute-done | bytes 2097184 | tf_op jit(solution)/shard_map/ppermute | solution.py:25
  162.9 47.8 %collective-permute-done.10 = bf16[2048,512]{1,0:T(8,128)(2,1)S(1)} collective-permute-done((bf16[2048,512]{1,0:T(8,128)(2,1)S(1)}, bf16[2048,512]{1,0:T(8,128)(2,1)S(1)}, u32[]{:S(2)}, u32[]{:S(2)}) %collective-permute-start.10) | collective-permute-done | bytes 2097184 | tf_op jit(solution)/shard_map/ppermute | solution.py:25
  212.1 46.9 %collective-permute-done.11 = bf16[2048,512]{1,0:T(8,128)(2,1)S(1)} collective-permute-done((bf16[2048,512]{1,0:T(8,128)(2,1)S(1)}, bf16[2048,512]{1,0:T(8,128)(2,1)S(1)}, u32[]{:S(2)}, u32[]{:S(2)}) %collective-permute-start.11) | collective-permute-done | bytes 2097184 | tf_op jit(solution)/shard_map/ppermute | solution.py:25
  260.3 46.2 %collective-permute-done.12 = bf16[2048,512]{1,0:T(8,128)(2,1)} collective-permute-done((bf16[2048,512]{1,0:T(8,128)(2,1)S(1)}, bf16[2048,512]{1,0:T(8,128)(2,1)}, u32[]{:S(2)}, u32[]{:S(2)}) %collective-permute-start.12) | collective-permute-done | bytes 2097184 | tf_op jit(solution)/shard_map/ppermute | solution.py:25
  306.5 2.4 copy.10
  309.0 43.0 %collective-permute-done.13 = bf16[2048,512]{1,0:T(8,128)(2,1)} collective-permute-done((bf16[2048,512]{1,0:T(8,128)(2,1)}, bf16[2048,512]{1,0:T(8,128)(2,1)}, u32[]{:S(2)}, u32[]{:S(2)}) %collective-permute-start.13) | collective-permute-done | bytes 2097184 | tf_op jit(solution)/shard_map/ppermute | solution.py:25
  352.0 3.1 constant_dynamic-update-slice_fusion.7
  355.2 3.1 constant_dynamic-update-slice_fusion.6
  358.2 3.1 constant_dynamic-update-slice_fusion.5
  361.4 3.1 constant_dynamic-update-slice_fusion.4
  370.6 15.0 %fusion.8 = bf16[2048,512]{0,1:T(8,128)(2,1)} fusion(bf16[1,4096,512]{1,2,0:T(8,128)(2,1)} %all-gather.9.cloned.1.call-done, s32[]{:T(128)S(6)} %select_n.40, bf16[2048,4096]{1,0:T(8,128)(2,1)} %constant_dynamic-update-slice_fusion), kind=kOutput, calls=%fused_computation.15 | convolution fusion | flops 8624537600 | bytes 23068676 | tf_op jit(solution)/shard_map/dot_general | solution.py:29
  385.6 45.7 %collective-permute-done.14 = bf16[2048,512]{0,1:T(8,128)(2,1)S(1)} collective-permute-done((bf16[2048,512]{0,1:T(8,128)(2,1)}, bf16[2048,512]{0,1:T(8,128)(2,1)S(1)}, u32[]{:S(2)}, u32[]{:S(2)}) %collective-permute-start.14) | collective-permute-done | bytes 2097184 | tf_op jit(solution)/shard_map/ppermute | solution.py:25
  431.3 45.9 %collective-permute-done.15 = bf16[2048,512]{0,1:T(8,128)(2,1)S(1)} collective-permute-done((bf16[2048,512]{0,1:T(8,128)(2,1)S(1)}, bf16[2048,512]{0,1:T(8,128)(2,1)S(1)}, u32[]{:S(2)}, u32[]{:S(2)}) %collective-permute-start.15) | collective-permute-done | bytes 2097184 | tf_op jit(solution)/shard_map/ppermute | solution.py:25
  477.2 2.5 collective-permute-start
  479.7 48.7 %collective-permute-done.16 = bf16[2048,512]{0,1:T(8,128)(2,1)S(1)} collective-permute-done((bf16[2048,512]{0,1:T(8,128)(2,1)S(1)}, bf16[2048,512]{0,1:T(8,128)(2,1)S(1)}, u32[]{:S(2)}, u32[]{:S(2)}) %collective-permute-start.16) | collective-permute-done | bytes 2097184 | tf_op jit(solution)/shard_map/ppermute | solution.py:25
  528.4 45.0 %collective-permute-done = bf16[2048,512]{0,1:T(8,128)(2,1)} collective-permute-done((bf16[2048,512]{0,1:T(8,128)(2,1)S(1)}, bf16[2048,512]{0,1:T(8,128)(2,1)}, u32[]{:S(2)}, u32[]{:S(2)}) %collective-permute-start) | collective-permute-done | bytes 2097184 | tf_op jit(solution)/shard_map/ppermute | solution.py:25
  573.4 44.9 %collective-permute-done.17 = bf16[2048,512]{0,1:T(8,128)(2,1)} collective-permute-done((bf16[2048,512]{0,1:T(8,128)(2,1)S(1)}, bf16[2048,512]{0,1:T(8,128)(2,1)}, u32[]{:S(2)}, u32[]{:S(2)}) %collective-permute-start.17) | collective-permute-done | bytes 2097184 | tf_op jit(solution)/shard_map/ppermute | solution.py:25
  618.4 44.9 %collective-permute-done.1 = bf16[2048,512]{0,1:T(8,128)(2,1)} collective-permute-done((bf16[2048,512]{0,1:T(8,128)(2,1)}, bf16[2048,512]{0,1:T(8,128)(2,1)}, u32[]{:S(2)}, u32[]{:S(2)}) %collective-permute-start.1) | collective-permute-done | bytes 2097184 | tf_op jit(solution)/shard_map/ppermute | solution.py:25
  663.3 44.9 %collective-permute-done.18 = bf16[2048,512]{0,1:T(8,128)(2,1)} collective-permute-done((bf16[2048,512]{0,1:T(8,128)(2,1)}, bf16[2048,512]{0,1:T(8,128)(2,1)}, u32[]{:S(2)}, u32[]{:S(2)}) %collective-permute-start.18) | collective-permute-done | bytes 2097184 | tf_op jit(solution)/shard_map/ppermute | solution.py:25
  708.2 44.9 %collective-permute-done.2 = bf16[2048,512]{0,1:T(8,128)(2,1)} collective-permute-done((bf16[2048,512]{0,1:T(8,128)(2,1)}, bf16[2048,512]{0,1:T(8,128)(2,1)}, u32[]{:S(2)}, u32[]{:S(2)}) %collective-permute-start.2) | collective-permute-done | bytes 2097184 | tf_op jit(solution)/shard_map/ppermute | solution.py:25
  753.2 44.9 %collective-permute-done.19 = bf16[2048,512]{0,1:T(8,128)(2,1)} collective-permute-done((bf16[2048,512]{0,1:T(8,128)(2,1)}, bf16[2048,512]{0,1:T(8,128)(2,1)}, u32[]{:S(2)}, u32[]{:S(2)}) %collective-permute-start.19) | collective-permute-done | bytes 2097184 | tf_op jit(solution)/shard_map/ppermute | solution.py:25
  798.1 3.3 collective-permute-start.21
  801.4 41.6 %collective-permute-done.3 = bf16[2048,512]{0,1:T(8,128)(2,1)} collective-permute-done((bf16[2048,512]{0,1:T(8,128)(2,1)}, bf16[2048,512]{0,1:T(8,128)(2,1)}, u32[]{:S(2)}, u32[]{:S(2)}) %collective-permute-start.3) | collective-permute-done | bytes 2097184 | tf_op jit(solution)/shard_map/ppermute | solution.py:25
  843.1 44.9 %collective-permute-done.20 = bf16[2048,512]{0,1:T(8,128)(2,1)} collective-permute-done((bf16[2048,512]{0,1:T(8,128)(2,1)}, bf16[2048,512]{0,1:T(8,128)(2,1)}, u32[]{:S(2)}, u32[]{:S(2)}) %collective-permute-start.20) | collective-permute-done | bytes 2097184 | tf_op jit(solution)/shard_map/ppermute | solution.py:25
  889.7 1.7 constant_dynamic-update-slice_fusion.14
  891.5 1.7 constant_dynamic-update-slice_fusion.13
  893.2 1.7 constant_dynamic-update-slice_fusion.12
  896.0 5.7 copy-done.17
  901.7 15.4 %fusion.19 = bf16[2048,512]{0,1:T(8,128)(2,1)} fusion(bf16[2048,512]{0,1:T(8,128)(2,1)} %fusion.8, bf16[4096,512]{0,1:T(8,128)(2,1)} %collective-permute-done.21, pred[]{:T(512)S(6)} %ge.3, s32[]{:T(128)S(6)} %select_n.40, bf16[2048,4096]{0,1:T(8,128)(2,1)} %copy-done.17), kind=kOutput, calls=%fused_computation.19 | convolution fusion | flops 8625586176 | bytes 25165828 | tf_op jit(solution)/shard_map/dot_general | solution.py:29
  917.1 9.9 collective-permute-done.4
  927.3 46.0 %collective-permute-done.5 = bf16[2048,512]{0,1:T(8,128)(2,1)} collective-permute-done((bf16[2048,512]{0,1:T(8,128)(2,1)}, bf16[2048,512]{0,1:T(8,128)(2,1)}, u32[]{:S(2)}, u32[]{:S(2)}) %collective-permute-start.5) | collective-permute-done | bytes 2097184 | tf_op jit(solution)/shard_map/ppermute | solution.py:25
  973.3 3.4 collective-permute-start.22
  976.6 42.0 %collective-permute-done.6 = bf16[2048,512]{0,1:T(8,128)(2,1)} collective-permute-done((bf16[2048,512]{0,1:T(8,128)(2,1)}, bf16[2048,512]{0,1:T(8,128)(2,1)}, u32[]{:S(2)}, u32[]{:S(2)}) %collective-permute-start.6) | collective-permute-done | bytes 2097184 | tf_op jit(solution)/shard_map/ppermute | solution.py:25
  1018.7 3.2 constant_dynamic-update-slice_fusion.23
  1021.9 3.2 constant_dynamic-update-slice_fusion.22
  1025.0 3.2 constant_dynamic-update-slice_fusion.21
  1028.2 3.2 constant_dynamic-update-slice_fusion.20
  1031.4 3.2 constant_dynamic-update-slice_fusion.19
  1034.6 3.3 constant_dynamic-update-slice_fusion.18
  1037.9 3.1 constant_dynamic-update-slice_fusion.17
  1042.6 15.6 %fusion.18 = bf16[1,2048,512]{1,2,0:T(8,128)(2,1)} fusion(bf16[2048,512]{0,1:T(8,128)(2,1)} %fusion.8, bf16[4096,512]{0,1:T(8,128)(2,1)} %collective-permute-done.22, pred[]{:T(512)S(6)} %gt.4, s32[]{:T(128)S(6)} %select_n.40, bf16[2048,4096]{0,1:T(8,128)(2,1)} %copy-done.17), kind=kOutput, calls=%fused_computation.18 | convolution fusion | flops 8627683328 | bytes 25165828 | tf_op jit(solution)/shard_map/dot_general | solution.py:29
  1058.2 15.3 %fusion.15 = bf16[1,2048,512]{1,2,0:T(8,128)(2,1)} fusion(bf16[4096,512]{0,1:T(8,128)(2,1)} %collective-permute-done.22, s32[]{:T(128)S(6)} %select_n.40, bf16[2048,4096]{0,1:T(8,128)(2,1)} %constant_dynamic-update-slice_fusion.16, pred[]{:T(512)S(6)} %gt.4, bf16[1,2048,512]{1,2,0:T(8,128)(2,1)S(1)} %copy-done), kind=kOutput, calls=%fused_computation.17 | convolution fusion | flops 8627683328 | bytes 25165828 | tf_op jit(solution)/shard_map/dot_general | solution.py:29
  1073.5 4.6 pad_maximum_fusion
  1078.0 6.2 copy.6
  (75 shorter events, 17.6 us)
Async XLA Ops:
  6.5 364.0 %all-gather.9.cloned.1.call-start = ((), (), s32[]{:S(2)}) async-start(), calls=%async_computation.2 | async-start | bytes 6291456 | tf_op jit(solution)/shard_map/all_gather | solution.py:17
  9.0 51.7 %collective-permute-start.7 = (bf16[2048,512]{1,0:T(8,128)(2,1)S(1)}, bf16[2048,512]{1,0:T(8,128)(2,1)S(1)}, u32[]{:S(2)}, u32[]{:S(2)}) collective-permute-start(bf16[2048,512]{1,0:T(8,128)(2,1)S(1)} %get-tuple-element.6), channel_id=1, source_target_pairs={{0,2},{2,4},{4,6},{6,8},{8,10},{10,12},{12,14},{14,0},{1,3},{3,5},... | collective-permute-start | bytes 6291464 | tf_op jit(solution)/shard_map/ppermute | solution.py:25
  60.7 1.4 copy-start.3
  62.1 49.5 %collective-permute-start.8 = (bf16[2048,512]{1,0:T(8,128)(2,1)S(1)}, bf16[2048,512]{1,0:T(8,128)(2,1)S(1)}, u32[]{:S(2)}, u32[]{:S(2)}) collective-permute-start(bf16[2048,512]{1,0:T(8,128)(2,1)S(1)} %collective-permute-done.7), channel_id=1, source_target_pairs={{0,2},{2,4},{4,6},{6,8},{8,10},{10,12},{12,14},{14,0},{1,3},{3,5},... | collective-permute-start | bytes 6291464 | tf_op jit(solution)/shard_map/ppermute | solution.py:25
  111.6 1.4 copy-start.7
  113.0 48.6 %collective-permute-start.9 = (bf16[2048,512]{1,0:T(8,128)(2,1)S(1)}, bf16[2048,512]{1,0:T(8,128)(2,1)S(1)}, u32[]{:S(2)}, u32[]{:S(2)}) collective-permute-start(bf16[2048,512]{1,0:T(8,128)(2,1)S(1)} %collective-permute-done.8), channel_id=1, source_target_pairs={{0,2},{2,4},{4,6},{6,8},{8,10},{10,12},{12,14},{14,0},{1,3},{3,5},... | collective-permute-start | bytes 6291464 | tf_op jit(solution)/shard_map/ppermute | solution.py:25
  161.6 1.3 copy-start.11
  162.9 47.8 %collective-permute-start.10 = (bf16[2048,512]{1,0:T(8,128)(2,1)S(1)}, bf16[2048,512]{1,0:T(8,128)(2,1)S(1)}, u32[]{:S(2)}, u32[]{:S(2)}) collective-permute-start(bf16[2048,512]{1,0:T(8,128)(2,1)S(1)} %collective-permute-done.9), channel_id=1, source_target_pairs={{0,2},{2,4},{4,6},{6,8},{8,10},{10,12},{12,14},{14,0},{1,3},{3,5},... | collective-permute-start | bytes 6291464 | tf_op jit(solution)/shard_map/ppermute | solution.py:25
  210.7 1.4 copy-start.15
  212.1 46.9 %collective-permute-start.11 = (bf16[2048,512]{1,0:T(8,128)(2,1)S(1)}, bf16[2048,512]{1,0:T(8,128)(2,1)S(1)}, u32[]{:S(2)}, u32[]{:S(2)}) collective-permute-start(bf16[2048,512]{1,0:T(8,128)(2,1)S(1)} %collective-permute-done.10), channel_id=1, source_target_pairs={{0,2},{2,4},{4,6},{6,8},{8,10},{10,12},{12,14},{14,0},{1,3},{3,5},... | collective-permute-start | bytes 6291464 | tf_op jit(solution)/shard_map/ppermute | solution.py:25
  259.0 1.3 copy-start.16
  260.3 46.2 %collective-permute-start.12 = (bf16[2048,512]{1,0:T(8,128)(2,1)S(1)}, bf16[2048,512]{1,0:T(8,128)(2,1)}, u32[]{:S(2)}, u32[]{:S(2)}) collective-permute-start(bf16[2048,512]{1,0:T(8,128)(2,1)S(1)} %collective-permute-done.11), channel_id=1, source_target_pairs={{0,2},{2,4},{4,6},{6,8},{8,10},{10,12},{12,14},{14,0},{1,3},{3,5},... | collective-permute-start | bytes 6291464 | tf_op jit(solution)/shard_map/ppermute | solution.py:25
  306.5 45.5 %collective-permute-start.13 = (bf16[2048,512]{1,0:T(8,128)(2,1)}, bf16[2048,512]{1,0:T(8,128)(2,1)}, u32[]{:S(2)}, u32[]{:S(2)}) collective-permute-start(bf16[2048,512]{1,0:T(8,128)(2,1)} %collective-permute-done.12), channel_id=1, source_target_pairs={{0,2},{2,4},{4,6},{6,8},{8,10},{10,12},{12,14},{14,0},{1,3},{3,5},... | collective-permute-start | bytes 6291464 | tf_op jit(solution)/shard_map/ppermute | solution.py:25
  308.9 58.7 %copy-start.4 = (bf16[2048,512]{1,0:T(8,128)(2,1)S(1)}, bf16[2048,512]{1,0:T(8,128)(2,1)}, u32[]{:S(2)}) copy-start(bf16[2048,512]{1,0:T(8,128)(2,1)} %copy-done.3) | copy-start | bytes 6291460
  308.9 489.2 %all-gather.5.cloned.1.call-start = ((), (), s32[]{:S(2)}) async-start(), calls=%async_computation | async-start | bytes 6291456 | tf_op jit(solution)/shard_map/all_gather | solution.py:17
  309.0 55.5 %copy-start.12 = (bf16[2048,512]{1,0:T(8,128)(2,1)S(1)}, bf16[2048,512]{1,0:T(8,128)(2,1)}, u32[]{:S(2)}) copy-start(bf16[2048,512]{1,0:T(8,128)(2,1)} %copy-done.11) | copy-start | bytes 6291460
  309.0 57.1 %copy-start.8 = (bf16[2048,512]{1,0:T(8,128)(2,1)S(1)}, bf16[2048,512]{1,0:T(8,128)(2,1)}, u32[]{:S(2)}) copy-start(bf16[2048,512]{1,0:T(8,128)(2,1)} %copy-done.7) | copy-start | bytes 6291460
  309.0 60.1 %copy-start.1 = (bf16[2,2048,512]{2,1,0:T(8,128)(2,1)S(1)}, bf16[2,2048,512]{2,1,0:T(8,128)(2,1)}, u32[]{:S(2)}) copy-start(bf16[2,2048,512]{2,1,0:T(8,128)(2,1)} %param.3) | copy-start | bytes 12582916
  370.6 106.6 %copy-start = (bf16[1,2048,512]{1,2,0:T(8,128)(2,1)S(1)}, bf16[1,2048,512]{1,2,0:T(8,128)(2,1)}, u32[]{:S(2)}) copy-start(bf16[1,2048,512]{1,2,0:T(8,128)(2,1)} %copy.10) | copy-start | bytes 6291460
  385.6 45.7 %collective-permute-start.14 = (bf16[2048,512]{0,1:T(8,128)(2,1)}, bf16[2048,512]{0,1:T(8,128)(2,1)S(1)}, u32[]{:S(2)}, u32[]{:S(2)}) collective-permute-start(bf16[2048,512]{0,1:T(8,128)(2,1)} %fusion.8), channel_id=1, source_target_pairs={{0,2},{2,4},{4,6},{6,8},{8,10},{10,12},{12,14},{14,0},{1,3},{3,5},... | collective-permute-start | bytes 6291464 | tf_op jit(solution)/shard_map/ppermute | solution.py:25
  431.3 142.2 %copy-start.5 = (bf16[2048,512]{0,1:T(8,128)(2,1)}, bf16[2048,512]{0,1:T(8,128)(2,1)S(1)}, u32[]{:S(2)}) copy-start(bf16[2048,512]{0,1:T(8,128)(2,1)S(1)} %collective-permute-done.14) | copy-start | bytes 6291460
  431.3 45.9 %collective-permute-start.15 = (bf16[2048,512]{0,1:T(8,128)(2,1)S(1)}, bf16[2048,512]{0,1:T(8,128)(2,1)S(1)}, u32[]{:S(2)}, u32[]{:S(2)}) collective-permute-start(bf16[2048,512]{0,1:T(8,128)(2,1)S(1)} %collective-permute-done.14), channel_id=1, source_target_pairs={{0,2},{2,4},{4,6},{6,8},{8,10},{10,12},{12,14},{14,0},{1,3},{3,5},... | collective-permute-start | bytes 6291464 | tf_op jit(solution)/shard_map/ppermute | solution.py:25
  477.2 96.3 %copy-start.9 = (bf16[2048,512]{0,1:T(8,128)(2,1)}, bf16[2048,512]{0,1:T(8,128)(2,1)S(1)}, u32[]{:S(2)}) copy-start(bf16[2048,512]{0,1:T(8,128)(2,1)S(1)} %collective-permute-done.15) | copy-start | bytes 6291460
  477.2 51.2 %collective-permute-start.16 = (bf16[2048,512]{0,1:T(8,128)(2,1)S(1)}, bf16[2048,512]{0,1:T(8,128)(2,1)S(1)}, u32[]{:S(2)}, u32[]{:S(2)}) collective-permute-start(bf16[2048,512]{0,1:T(8,128)(2,1)S(1)} %collective-permute-done.15), channel_id=1, source_target_pairs={{0,2},{2,4},{4,6},{6,8},{8,10},{10,12},{12,14},{14,0},{1,3},{3,5},... | collective-permute-start | bytes 6291464 | tf_op jit(solution)/shard_map/ppermute | solution.py:25
  477.2 96.2 %collective-permute-start = (bf16[2048,512]{0,1:T(8,128)(2,1)S(1)}, bf16[2048,512]{0,1:T(8,128)(2,1)}, u32[]{:S(2)}, u32[]{:S(2)}) collective-permute-start(bf16[2048,512]{0,1:T(8,128)(2,1)S(1)} %bitcast.19), channel_id=1, source_target_pairs={{0,2},{2,4},{4,6},{6,8},{8,10},{10,12},{12,14},{14,0},{1,3},{3,5},... | collective-permute-start | bytes 6291464 | tf_op jit(solution)/shard_map/ppermute | solution.py:25
  528.4 90.0 %copy-start.13 = (bf16[2048,512]{0,1:T(8,128)(2,1)}, bf16[2048,512]{0,1:T(8,128)(2,1)S(1)}, u32[]{:S(2)}) copy-start(bf16[2048,512]{0,1:T(8,128)(2,1)S(1)} %collective-permute-done.16) | copy-start | bytes 6291460
  528.4 90.0 %collective-permute-start.17 = (bf16[2048,512]{0,1:T(8,128)(2,1)S(1)}, bf16[2048,512]{0,1:T(8,128)(2,1)}, u32[]{:S(2)}, u32[]{:S(2)}) collective-permute-start(bf16[2048,512]{0,1:T(8,128)(2,1)S(1)} %collective-permute-done.16), channel_id=1, source_target_pairs={{0,2},{2,4},{4,6},{6,8},{8,10},{10,12},{12,14},{14,0},{1,3},{3,5},... | collective-permute-start | bytes 6291464 | tf_op jit(solution)/shard_map/ppermute | solution.py:25
  573.4 89.9 %collective-permute-start.1 = (bf16[2048,512]{0,1:T(8,128)(2,1)}, bf16[2048,512]{0,1:T(8,128)(2,1)}, u32[]{:S(2)}, u32[]{:S(2)}) collective-permute-start(bf16[2048,512]{0,1:T(8,128)(2,1)} %collective-permute-done), channel_id=1, source_target_pairs={{0,2},{2,4},{4,6},{6,8},{8,10},{10,12},{12,14},{14,0},{1,3},{3,5},... | collective-permute-start | bytes 6291464 | tf_op jit(solution)/shard_map/ppermute | solution.py:25
  618.3 89.9 %collective-permute-start.18 = (bf16[2048,512]{0,1:T(8,128)(2,1)}, bf16[2048,512]{0,1:T(8,128)(2,1)}, u32[]{:S(2)}, u32[]{:S(2)}) collective-permute-start(bf16[2048,512]{0,1:T(8,128)(2,1)} %collective-permute-done.17), channel_id=1, source_target_pairs={{0,2},{2,4},{4,6},{6,8},{8,10},{10,12},{12,14},{14,0},{1,3},{3,5},... | collective-permute-start | bytes 6291464 | tf_op jit(solution)/shard_map/ppermute | solution.py:25
  618.4 354.9 %all-gather.7.cloned.1.call-start = ((), (), s32[]{:S(2)}) async-start(), calls=%async_computation.1 | async-start | bytes 6291456 | tf_op jit(solution)/shard_map/all_gather | solution.py:17
  663.3 89.9 %collective-permute-start.2 = (bf16[2048,512]{0,1:T(8,128)(2,1)}, bf16[2048,512]{0,1:T(8,128)(2,1)}, u32[]{:S(2)}, u32[]{:S(2)}) collective-permute-start(bf16[2048,512]{0,1:T(8,128)(2,1)} %collective-permute-done.1), channel_id=1, source_target_pairs={{0,2},{2,4},{4,6},{6,8},{8,10},{10,12},{12,14},{14,0},{1,3},{3,5},... | collective-permute-start | bytes 6291464 | tf_op jit(solution)/shard_map/ppermute | solution.py:25
  708.2 89.9 %collective-permute-start.19 = (bf16[2048,512]{0,1:T(8,128)(2,1)}, bf16[2048,512]{0,1:T(8,128)(2,1)}, u32[]{:S(2)}, u32[]{:S(2)}) collective-permute-start(bf16[2048,512]{0,1:T(8,128)(2,1)} %collective-permute-done.18), channel_id=1, source_target_pairs={{0,2},{2,4},{4,6},{6,8},{8,10},{10,12},{12,14},{14,0},{1,3},{3,5},... | collective-permute-start | bytes 6291464 | tf_op jit(solution)/shard_map/ppermute | solution.py:25
  753.2 89.9 %collective-permute-start.3 = (bf16[2048,512]{0,1:T(8,128)(2,1)}, bf16[2048,512]{0,1:T(8,128)(2,1)}, u32[]{:S(2)}, u32[]{:S(2)}) collective-permute-start(bf16[2048,512]{0,1:T(8,128)(2,1)} %collective-permute-done.2), channel_id=1, source_target_pairs={{0,2},{2,4},{4,6},{6,8},{8,10},{10,12},{12,14},{14,0},{1,3},{3,5},... | collective-permute-start | bytes 6291464 | tf_op jit(solution)/shard_map/ppermute | solution.py:25
  798.1 89.9 %collective-permute-start.20 = (bf16[2048,512]{0,1:T(8,128)(2,1)}, bf16[2048,512]{0,1:T(8,128)(2,1)}, u32[]{:S(2)}, u32[]{:S(2)}) collective-permute-start(bf16[2048,512]{0,1:T(8,128)(2,1)} %collective-permute-done.19), channel_id=1, source_target_pairs={{0,2},{2,4},{4,6},{6,8},{8,10},{10,12},{12,14},{14,0},{1,3},{3,5},... | collective-permute-start | bytes 6291464 | tf_op jit(solution)/shard_map/ppermute | solution.py:25
  798.1 103.6 %collective-permute-start.21 = (bf16[4096,512]{0,1:T(8,128)(2,1)}, bf16[4096,512]{0,1:T(8,128)(2,1)}, u32[]{:S(2)}, u32[]{:S(2)}) collective-permute-start(bf16[4096,512]{0,1:T(8,128)(2,1)} %all-gather.5.cloned.1.call-done), channel_id=1, source_target_pairs={{0,1},{2,3},{4,5},{6,7},{8,9},{10,11},{12,13},{14,15},{16,17},{18,... | collective-permute-start | bytes 12582920 | tf_op jit(solution)/shard_map/ppermute | solution.py:13
  801.4 93.5 %copy-start.14 = (bf16[2048,512]{0,1:T(8,128)(2,1)S(1)}, bf16[2048,512]{0,1:T(8,128)(2,1)}, u32[]{:S(2)}) copy-start(bf16[2048,512]{0,1:T(8,128)(2,1)} %copy-done.13) | copy-start | bytes 6291460
  801.4 93.8 %copy-start.10 = (bf16[2048,512]{0,1:T(8,128)(2,1)S(1)}, bf16[2048,512]{0,1:T(8,128)(2,1)}, u32[]{:S(2)}) copy-start(bf16[2048,512]{0,1:T(8,128)(2,1)} %copy-done.9) | copy-start | bytes 6291460
  801.4 94.0 %copy-start.6 = (bf16[2048,512]{0,1:T(8,128)(2,1)S(1)}, bf16[2048,512]{0,1:T(8,128)(2,1)}, u32[]{:S(2)}) copy-start(bf16[2048,512]{0,1:T(8,128)(2,1)} %copy-done.5) | copy-start | bytes 6291460
  801.4 94.3 %copy-start.2 = (bf16[2048,512]{0,1:T(8,128)(2,1)S(1)}, bf16[2048,512]{0,1:T(8,128)(2,1)}, u32[]{:S(2)}) copy-start(bf16[2048,512]{0,1:T(8,128)(2,1)} %fusion.8) | copy-start | bytes 6291460
  843.1 84.0 %collective-permute-start.4 = (bf16[2048,512]{0,1:T(8,128)(2,1)}, bf16[2048,512]{0,1:T(8,128)(2,1)}, u32[]{:S(2)}, u32[]{:S(2)}) collective-permute-start(bf16[2048,512]{0,1:T(8,128)(2,1)} %collective-permute-done.3), channel_id=1, source_target_pairs={{0,2},{2,4},{4,6},{6,8},{8,10},{10,12},{12,14},{14,0},{1,3},{3,5},... | collective-permute-start | bytes 6291464 | tf_op jit(solution)/shard_map/ppermute | solution.py:25
  895.9 5.8 copy-start.17
  927.0 46.3 %collective-permute-start.5 = (bf16[2048,512]{0,1:T(8,128)(2,1)}, bf16[2048,512]{0,1:T(8,128)(2,1)}, u32[]{:S(2)}, u32[]{:S(2)}) collective-permute-start(bf16[2048,512]{0,1:T(8,128)(2,1)} %collective-permute-done.4), channel_id=1, source_target_pairs={{0,2},{2,4},{4,6},{6,8},{8,10},{10,12},{12,14},{14,0},{1,3},{3,5},... | collective-permute-start | bytes 6291464 | tf_op jit(solution)/shard_map/ppermute | solution.py:25
  973.3 45.4 %collective-permute-start.6 = (bf16[2048,512]{0,1:T(8,128)(2,1)}, bf16[2048,512]{0,1:T(8,128)(2,1)}, u32[]{:S(2)}, u32[]{:S(2)}) collective-permute-start(bf16[2048,512]{0,1:T(8,128)(2,1)} %collective-permute-done.5), channel_id=1, source_target_pairs={{0,2},{2,4},{4,6},{6,8},{8,10},{10,12},{12,14},{14,0},{1,3},{3,5},... | collective-permute-start | bytes 6291464 | tf_op jit(solution)/shard_map/ppermute | solution.py:25
  973.3 69.3 %collective-permute-start.22 = (bf16[4096,512]{0,1:T(8,128)(2,1)}, bf16[4096,512]{0,1:T(8,128)(2,1)}, u32[]{:S(2)}, u32[]{:S(2)}) collective-permute-start(bf16[4096,512]{0,1:T(8,128)(2,1)} %all-gather.7.cloned.1.call-done), channel_id=1, source_target_pairs={{0,1},{2,3},{4,5},{6,7},{8,9},{10,11},{12,13},{14,15},{16,17},{18,... | collective-permute-start | bytes 12582920 | tf_op jit(solution)/shard_map/ppermute | solution.py:13
Sparse Core Ops, SparseCore 0:
  309.0 57.1 all-gather.8
  618.5 57.3 all-gather.4
  917.2 53.4 all-gather.6
